TPU v7x, 32 devices: a whole 2x2x4 slice. The times are simulated.
32 devices in a mesh: groups: 2 (over y), row: 4 (over z), col: 2 (over x), rep: 2 (over core).
Axes of the slice: x: 2, y: 2, z: 4, core: 2. Of those that a mesh axis runs over, the one named last changes fastest.
Arguments:
- kernel: float32 [32768, 16384], P(('groups', 'row'), ('col', 'rep')), parts along dimension 0, may hold values from 0 to 2, as said below
- source: float32 [64, 16384], P('groups', 'row'), parts along dimension 0, may hold values from 0.5 to 2, as said below
- target: float32 [64, 16384], P('groups', ('col', 'rep')), parts along dimension 0, may hold values from 0.5 to 2, as said below
Outputs:
- left_scale: float32 [64, 16384], P('groups', 'row'), parts along dimension 0
- right_scale: float32 [64, 16384], P('groups', ('col', 'rep')), parts along dimension 0
- errors: float32 [6, 32], P('groups'), parts along dimension 0
There are 2 independent parts, one for each index of `groups`. A program takes and returns all parts, laid end to end along the dimension named above; each array names one. Nothing has to cross between parts.
Inputs may be any that keep to these rules, and one draw needn't show every extreme that they name: `kernel`: every entry is positive. `source`: every entry is positive. `target`: every entry is positive.
All inputs are finite; a program needn't handle non-finite values.
Results may differ from a plain program's by a relative error of at most 0.0001.
Values sent between devices are 32-bit elements; how exact they have to be, the bound alone decides.
A program may use at most 128 MiB of HBM per device.

v0:
```python
import jax
import jax.numpy as jnp
from jax import lax
from jax.sharding import PartitionSpec as P

N = 16384
ITERS = 3


def local(kernel, source, target):
    columns = kernel.shape[1]
    right_scale = jnp.ones(target.shape, jnp.float32)
    left_scale = source
    share = columns // lax.axis_size("row")
    offset = lax.axis_index("row") * share
    errors = []
    for step in range(ITERS):
        partial_value = lax.dot_general(
            right_scale, kernel, (((1,), (1,)), ((), ())), precision=lax.Precision.HIGHEST
        )
        left_scale = source / lax.psum(partial_value, ("col", "rep"))
        back = jnp.dot(left_scale, kernel, precision=lax.Precision.HIGHEST)
        old_piece = lax.dynamic_slice_in_dim(right_scale, offset, share, 1)
        target_piece = lax.dynamic_slice_in_dim(target, offset, share, 1)
        total_piece = lax.psum_scatter(back, "row", scatter_dimension=1, tiled=True)
        right_scale = lax.all_gather(target_piece / total_piece, "row", axis=1, tiled=True)
        term = jnp.sum(jnp.abs(old_piece * total_piece - target_piece), axis=1) / N
        errors.append(lax.psum(term, ("row", "col", "rep")))
    stacked = jnp.stack(errors)
    return (left_scale, right_scale, stacked)


def solution(mesh):
    return jax.shard_map(
        local,
        mesh=mesh,
        in_specs=(
            P(("groups", "row"), ("col", "rep")),
            P("groups", "row"),
            P("groups", ("col", "rep")),
        ),
        out_specs=(P("groups", "row"), P("groups", ("col", "rep")), P("groups", None)),
        check_vma=False,
    )
```

profile of v0, /device:TPU:0, one launch (start us, length us, event | category | flops | bytes accessed | tf_op | source)
XLA Modules:
  0.0 597.1 jit_solution(12538912805392526422)
XLA Ops:
  7.2 0.0 copy-start
  7.2 0.0 all-reduce.5.cloned.1.call-start
  7.2 66.4 %fusion.4 = f32[32,4096]{1,0:T(8,128)} fusion(f32[4096,4096]{1,0:T(8,128)} %param.3), kind=kOutput, calls=%fused_computation.4 | convolution fusion | flops 6442450944 | bytes 67633152 | tf_op jit(solution)/shard_map/dot_general | solution.py:18
  73.7 0.0 copy-start.4
  73.7 0.0 all-reduce.5.cloned.1.call-update
  73.7 0.3 reduce-scatter.4.cloned.1.call-start
  74.0 36.0 %all-reduce.5.cloned.1.call-done = f32[32,4096]{1,0:T(8,128)} async-done(((f32[32,4096]{1,0:T(8,128)}), f32[32,4096]{1,0:T(8,128)}) %all-reduce.5.cloned.1.call-update) | async-done | bytes 524304 | tf_op jit(solution)/shard_map/psum | solution.py:21
  110.0 0.0 copy-done
  110.0 44.8 %fusion.2 = f32[32,4096]{1,0:T(8,128)} fusion(f32[4096,4096]{1,0:T(8,128)} %param.3, f32[32,4096]{1,0:T(8,128)S(1)} %copy-done, f32[32,4096]{1,0:T(8,128)} %all-reduce.5.cloned.1.call-done), kind=kOutput, calls=%fused_computation.2 | convolution fusion | flops 6442582016 | bytes 68681728 | tf_op jit(solution)/shard_map/dot_general | solution.py:22
  154.8 0.0 reduce-scatter.4.cloned.1.call-update
  154.9 0.0 all-reduce.7.cloned.1.call-start
  154.9 22.1 %reduce-scatter.4.cloned.1.call-done = f32[32,1024]{1,0:T(8,128)} async-done(((f32[32,4096]{1,0:T(8,128)}), f32[32,1024]{1,0:T(8,128)}) %reduce-scatter.4.cloned.1.call-update) | async-done | bytes 131088 | tf_op jit(solution)/shard_map/reduce_scatter | solution.py:25
  177.0 0.0 copy-done.4
  177.0 0.9 dynamic-slice_divide_fusion.2
  177.9 15.7 %all_gather.9 = f32[32,4096]{1,0:T(8,128)S(1)} all-gather(f32[32,1024]{1,0:T(8,128)S(1)} %dynamic-slice_divide_fusion.2), channel_id=1, replica_groups=mesh['groups'=2,'row'=4,'col'=2,'rep'=2] {'row'}, dimensions={1}, use_global_device_ids=true | all-gather | bytes 655360 | tf_op jit(solution)/shard_map/all_gather | solution.py:26
  193.7 66.5 %fusion.7 = f32[32,4096]{1,0:T(8,128)} fusion(f32[32,4096]{1,0:T(8,128)S(1)} %all_gather.9, f32[4096,4096]{1,0:T(8,128)} %param.3), kind=kOutput, calls=%fused_computation.17 | convolution fusion | flops 6442450944 | bytes 68157440 | tf_op jit(solution)/shard_map/dot_general | solution.py:18
  260.2 0.0 all-reduce.7.cloned.1.call-update
  260.2 0.2 reduce-scatter.6.cloned.1.call-start
  260.4 31.8 %all-reduce.7.cloned.1.call-done = f32[32,4096]{1,0:T(8,128)} async-done(((f32[32,4096]{1,0:T(8,128)}), f32[32,4096]{1,0:T(8,128)}) %all-reduce.7.cloned.1.call-update) | async-done | bytes 524304 | tf_op jit(solution)/shard_map/psum | solution.py:21
  292.2 44.8 %fusion = f32[32,4096]{1,0:T(8,128)} fusion(f32[4096,4096]{1,0:T(8,128)} %param.3, f32[32,4096]{1,0:T(8,128)S(1)} %copy-done, f32[32,4096]{1,0:T(8,128)} %all-reduce.7.cloned.1.call-done), kind=kOutput, calls=%fused_computation | convolution fusion | flops 6442582016 | bytes 68681728 | tf_op jit(solution)/shard_map/dot_general | solution.py:22
  337.0 0.0 reduce-scatter.6.cloned.1.call-update
  337.0 0.0 all-reduce.9.cloned.1.call-start
  337.1 22.0 %reduce-scatter.6.cloned.1.call-done = f32[32,1024]{1,0:T(8,128)} async-done(((f32[32,4096]{1,0:T(8,128)}), f32[32,1024]{1,0:T(8,128)}) %reduce-scatter.6.cloned.1.call-update) | async-done | bytes 131088 | tf_op jit(solution)/shard_map/reduce_scatter | solution.py:25
  359.1 0.9 dynamic-slice_divide_fusion.1
  360.0 15.7 %all_gather.10 = f32[32,4096]{1,0:T(8,128)S(1)} all-gather(f32[32,1024]{1,0:T(8,128)S(1)} %dynamic-slice_divide_fusion.1), channel_id=1, replica_groups=mesh['groups'=2,'row'=4,'col'=2,'rep'=2] {'row'}, dimensions={1}, use_global_device_ids=true | all-gather | bytes 655360 | tf_op jit(solution)/shard_map/all_gather | solution.py:26
  375.7 66.5 %fusion.8 = f32[32,4096]{1,0:T(8,128)} fusion(f32[32,4096]{1,0:T(8,128)S(1)} %all_gather.10, f32[4096,4096]{1,0:T(8,128)} %param.3), kind=kOutput, calls=%fused_computation.18 | convolution fusion | flops 6442450944 | bytes 68157440 | tf_op jit(solution)/shard_map/dot_general | solution.py:18
  442.2 0.0 copy-start.2
  442.2 0.0 copy-start.3
  442.2 0.0 all-reduce.9.cloned.1.call-update
  442.2 0.3 reduce-scatter.8.cloned.1.call-start
  442.5 31.6 %all-reduce.9.cloned.1.call-done = f32[32,4096]{1,0:T(8,128)} async-done(((f32[32,4096]{1,0:T(8,128)}), f32[32,4096]{1,0:T(8,128)}) %all-reduce.9.cloned.1.call-update) | async-done | bytes 524304 | tf_op jit(solution)/shard_map/psum | solution.py:21
  474.2 1.1 div.31
  475.3 0.0 copy-start.1
  475.3 45.0 %fusion.9 = f32[32,4096]{1,0:T(8,128)} fusion(f32[32,4096]{1,0:T(8,128)S(1)} %div.31, f32[4096,4096]{1,0:T(8,128)} %param.3), kind=kOutput, calls=%fused_computation.19 | convolution fusion | flops 6442450944 | bytes 68157440 | tf_op jit(solution)/shard_map/dot_general | solution.py:22
  520.3 0.0 reduce-scatter.8.cloned.1.call-update
  520.4 22.1 %reduce-scatter.8.cloned.1.call-done = f32[32,1024]{1,0:T(8,128)} async-done(((f32[32,4096]{1,0:T(8,128)}), f32[32,1024]{1,0:T(8,128)}) %reduce-scatter.8.cloned.1.call-update) | async-done | bytes 131088 | tf_op jit(solution)/shard_map/reduce_scatter | solution.py:25
  542.5 0.0 copy-done.2
  542.5 0.0 copy-done.3
  542.5 1.1 abs_reduce_fusion.2
  543.6 15.3 %all_gather.11 = f32[32,4096]{1,0:T(8,128)S(1)} all-gather(f32[32,1024]{1,0:T(8,128)S(1)} %get-tuple-element.9), channel_id=1, replica_groups=mesh['groups'=2,'row'=4,'col'=2,'rep'=2] {'row'}, dimensions={1}, use_global_device_ids=true | all-gather | bytes 655360 | tf_op jit(solution)/shard_map/all_gather | solution.py:26
  558.9 29.5 %all-reduce = (f32[1,32]{1,0:T(1,128)S(1)}, f32[1,32]{1,0:T(1,128)S(1)}, f32[1,32]{1,0:T(1,128)S(1)}) all-reduce(f32[1,32]{1,0:T(1,128)S(1)} %get-tuple-element.10, f32[1,32]{1,0:T(1,128)S(1)} %get-tuple-element.11, f32[1,32]{1,0:T(1,128)S(1)} %multiply_bitcast_fusion.2), channel_id=1, replica_groups=mesh['groups'=2,'row'=4,'col'=2,'rep'=2] {'row','col','rep'}, use_global_device_ids=true, to_apply=%region_11.0 | all-reduce | flops 96 | bytes 768 | tf_op jit(solution)/shard_map/psum | solution.py:28
  588.4 0.6 pad_maximum_fusion
  589.0 0.8 copy.10
  589.8 0.0 copy-done.1
  (2 shorter events, 0.0 us)
Async XLA Ops:
  7.2 102.8 %copy-start = (f32[32,4096]{1,0:T(8,128)S(1)}, f32[32,4096]{1,0:T(8,128)}, u32[]{:S(2)}) copy-start(f32[32,4096]{1,0:T(8,128)} %param.4) | copy-start | bytes 1572868
  7.2 102.8 %all-reduce.5.cloned.1.call-start = ((), (), s32[]{:S(2)}) async-start(), calls=%async_computation.3 | async-start | bytes 1048576 | tf_op jit(solution)/shard_map/psum | solution.py:21
  73.7 103.3 %copy-start.4 = (f32[32,4096]{1,0:T(8,128)S(1)}, f32[32,4096]{1,0:T(8,128)}, u32[]{:S(2)}) copy-start(f32[32,4096]{1,0:T(8,128)} %param.5) | copy-start | bytes 1572868
  73.7 103.3 %reduce-scatter.4.cloned.1.call-start = ((), (), s32[]{:S(2)}) async-start(), calls=%async_computation.4 | async-start | bytes 655360 | tf_op jit(solution)/shard_map/reduce_scatter | solution.py:25
  154.9 137.3 %all-reduce.7.cloned.1.call-start = ((), (), s32[]{:S(2)}) async-start(), calls=%async_computation.5 | async-start | bytes 1048576 | tf_op jit(solution)/shard_map/psum | solution.py:21
  260.2 98.9 %reduce-scatter.6.cloned.1.call-start = ((), (), s32[]{:S(2)}) async-start(), calls=%async_computation.6 | async-start | bytes 655360 | tf_op jit(solution)/shard_map/reduce_scatter | solution.py:25
  337.0 137.1 %all-reduce.9.cloned.1.call-start = ((), (), s32[]{:S(2)}) async-start(), calls=%async_computation.7 | async-start | bytes 1048576 | tf_op jit(solution)/shard_map/psum | solution.py:21
  442.2 100.3 %copy-start.2 = (f32[32,1024]{1,0:T(8,128)S(1)}, f32[32,1024]{1,0:T(8,128)}, u32[]{:S(2)}) copy-start(f32[32,1024]{1,0:T(8,128)} %reduce-scatter.4.cloned.1.call-done) | copy-start | bytes 393220
  442.2 100.3 %copy-start.3 = (f32[32,1024]{1,0:T(8,128)S(1)}, f32[32,1024]{1,0:T(8,128)}, u32[]{:S(2)}) copy-start(f32[32,1024]{1,0:T(8,128)} %reduce-scatter.6.cloned.1.call-done) | copy-start | bytes 393220
  442.2 100.2 %reduce-scatter.8.cloned.1.call-start = ((), (), s32[]{:S(2)}) async-start(), calls=%async_computation.8 | async-start | bytes 655360 | tf_op jit(solution)/shard_map/reduce_scatter | solution.py:25
  475.3 114.5 %copy-start.1 = (f32[32,4096]{1,0:T(8,128)}, f32[32,4096]{1,0:T(8,128)S(1)}, u32[]{:S(2)}) copy-start(f32[32,4096]{1,0:T(8,128)S(1)} %div.31) | copy-start | bytes 1572868
Sparse Core Ops, SparseCore 0:
  73.8 36.1 all-reduce.4
  155.0 21.9 reduce-scatter.3
  260.3 31.8 all-reduce.6
  337.1 21.9 reduce-scatter.5
  442.4 31.7 all-reduce.8
  520.5 21.9 reduce-scatter.7
where the time goes:
time: 606 us; the launch traced here: 597 us
  matrix products  334 us (55%)
  waiting for transfers between devices  166 us (27%)
  blocking collectives  76.2 us (13%)
  between operations  14.6 us (2%)
    dot_general x3, matrix products, local(): lax.dot_general(right_scale, kernel, (((1,), (1,)), ((), ())), precision=...  199 us
    dot_general x3, matrix products, local(): back = jnp.dot(left_scale, kernel, precision=lax.Precision.HIGHEST)  135 us
    psum x3, waiting for transfers between devices, local(): left_scale = source / lax.psum(partial_value, ('col', 'rep'))  99.4 us
    reduce_scatter x3, waiting for transfers between devices, local(): total_piece = lax.psum_scatter(back, 'row', scatter_dimension=1, tiled=True)  66.2 us
    all_gather x3, blocking collectives, local(): lax.all_gather(target_piece / total_piece, 'row', axis=1, tiled=True)  46.8 us
    psum x1, blocking collectives, local(): errors.append(lax.psum(term, ('row', 'col', 'rep')))  29.5 us
  transfers between devices with their start and end apart: 6, of which 6 were waited for; matrix products, arithmetic and copies ran while one was open for 0% of the time, Pallas kernels for 0%

commit v1 on v0

--- a/solution.py
+++ b/solution.py
@@ -18,7 +18,7 @@
         partial_value = lax.dot_general(
             right_scale, kernel, (((1,), (1,)), ((), ())), precision=lax.Precision.HIGHEST
         )
-        left_scale = source / lax.psum(partial_value, ("col", "rep"))
+        left_scale = source / lax.psum(lax.psum(partial_value, "rep"), "col")
         back = jnp.dot(left_scale, kernel, precision=lax.Precision.HIGHEST)
         old_piece = lax.dynamic_slice_in_dim(right_scale, offset, share, 1)
         target_piece = lax.dynamic_slice_in_dim(target, offset, share, 1)

time: 606 us -> 657 us (1.084)
  waiting for transfers between devices: 166 us -> 217 us
    psum x3 -> x6, waiting for transfers between devices: 99.4 us -> 151 us  [local(): left_scale = source / lax.psum(lax.psum(partial_value, 'rep'), 'col')]
  transfers between devices with their start and end apart: 6 -> 9, of which waited for: 6 -> 9; matrix products, arithmetic and copies ran while one was open for 0% -> 0% of each run, Pallas kernels for 0% -> 0%
where the time goes in v1:
time: 657 us; the launch traced here: 648 us
  matrix products  334 us (51%)
  waiting for transfers between devices  217 us (33%)
  blocking collectives  76.2 us (12%)
  between operations  14.3 us (2%)
    dot_general x3, matrix products, local(): lax.dot_general(right_scale, kernel, (((1,), (1,)), ((), ())), precision=...  199 us
    psum x6, waiting for transfers between devices, local(): left_scale = source / lax.psum(lax.psum(partial_value, 'rep'), 'col')  151 us
    dot_general x3, matrix products, local(): back = jnp.dot(left_scale, kernel, precision=lax.Precision.HIGHEST)  135 us
    reduce_scatter x3, waiting for transfers between devices, local(): total_piece = lax.psum_scatter(back, 'row', scatter_dimension=1, tiled=True)  65.8 us
    all_gather x3, blocking collectives, local(): lax.all_gather(target_piece / total_piece, 'row', axis=1, tiled=True)  46.7 us
    psum x1, blocking collectives, local(): errors.append(lax.psum(term, ('row', 'col', 'rep')))  29.5 us
  transfers between devices with their start and end apart: 9, of which 9 were waited for; matrix products, arithmetic and copies ran while one was open for 0% of the time, Pallas kernels for 0%

profile of v1, /device:TPU:0, one launch (start us, length us, event | category | flops | bytes accessed | tf_op | source)
XLA Modules:
  0.0 648.4 jit_solution(8065400151995534304)
XLA Ops:
  7.2 0.0 copy-start
  7.2 0.0 all-reduce.8.cloned.1.call-start
  7.2 66.4 %fusion.4 = f32[32,4096]{1,0:T(8,128)} fusion(f32[4096,4096]{1,0:T(8,128)} %param.3), kind=kOutput, calls=%fused_computation.4 | convolution fusion | flops 6442450944 | bytes 67633152 | tf_op jit(solution)/shard_map/dot_general | solution.py:18
  73.7 0.0 all-reduce.8.cloned.1.call-update
  73.7 0.0 all-reduce.10.cloned.1.call-start
  73.7 21.4 %all-reduce.8.cloned.1.call-done = f32[32,4096]{1,0:T(8,128)} async-done(((f32[32,4096]{1,0:T(8,128)}), f32[32,4096]{1,0:T(8,128)}) %all-reduce.8.cloned.1.call-update) | async-done | bytes 524304 | tf_op jit(solution)/shard_map/psum | solution.py:21
  95.2 0.0 all-reduce.10.cloned.1.call-update
  95.2 0.3 reduce-scatter.4.cloned.1.call-start
  95.5 31.9 %all-reduce.10.cloned.1.call-done = f32[32,4096]{1,0:T(8,128)} async-done(((f32[32,4096]{1,0:T(8,128)}), f32[32,4096]{1,0:T(8,128)}) %all-reduce.10.cloned.1.call-update) | async-done | bytes 524304 | tf_op jit(solution)/shard_map/psum | solution.py:21
  127.4 0.0 copy-done
  127.4 44.8 %fusion.2 = f32[32,4096]{1,0:T(8,128)} fusion(f32[4096,4096]{1,0:T(8,128)} %param.3, f32[32,4096]{1,0:T(8,128)S(1)} %copy-done, f32[32,4096]{1,0:T(8,128)} %all-reduce.10.cloned.1.call-done), kind=kOutput, calls=%fused_computation.2 | convolution fusion | flops 6442582016 | bytes 68681728 | tf_op jit(solution)/shard_map/dot_general | solution.py:22
  172.2 0.0 reduce-scatter.4.cloned.1.call-update
  172.2 0.0 all-reduce.12.cloned.1.call-start
  172.3 21.9 %reduce-scatter.4.cloned.1.call-done = f32[32,1024]{1,0:T(8,128)} async-done(((f32[32,4096]{1,0:T(8,128)}), f32[32,1024]{1,0:T(8,128)}) %reduce-scatter.4.cloned.1.call-update) | async-done | bytes 131088 | tf_op jit(solution)/shard_map/reduce_scatter | solution.py:25
  194.2 0.0 copy-done.4
  194.2 0.9 dynamic-slice_divide_fusion.2
  195.1 15.8 %all_gather.9 = f32[32,4096]{1,0:T(8,128)S(1)} all-gather(f32[32,1024]{1,0:T(8,128)S(1)} %dynamic-slice_divide_fusion.2), channel_id=1, replica_groups=mesh['groups'=2,'row'=4,'col'=2,'rep'=2] {'row'}, dimensions={1}, use_global_device_ids=true | all-gather | bytes 655360 | tf_op jit(solution)/shard_map/all_gather | solution.py:26
  210.9 66.5 %fusion.7 = f32[32,4096]{1,0:T(8,128)} fusion(f32[32,4096]{1,0:T(8,128)S(1)} %all_gather.9, f32[4096,4096]{1,0:T(8,128)} %param.3), kind=kOutput, calls=%fused_computation.17 | convolution fusion | flops 6442450944 | bytes 68157440 | tf_op jit(solution)/shard_map/dot_general | solution.py:18
  277.4 0.0 all-reduce.12.cloned.1.call-update
  277.4 0.0 all-reduce.14.cloned.1.call-start
  277.5 17.2 %all-reduce.12.cloned.1.call-done = f32[32,4096]{1,0:T(8,128)} async-done(((f32[32,4096]{1,0:T(8,128)}), f32[32,4096]{1,0:T(8,128)}) %all-reduce.12.cloned.1.call-update) | async-done | bytes 524304 | tf_op jit(solution)/shard_map/psum | solution.py:21
  294.7 0.0 all-reduce.14.cloned.1.call-update
  294.7 0.2 reduce-scatter.6.cloned.1.call-start
  294.9 31.8 %all-reduce.14.cloned.1.call-done = f32[32,4096]{1,0:T(8,128)} async-done(((f32[32,4096]{1,0:T(8,128)}), f32[32,4096]{1,0:T(8,128)}) %all-reduce.14.cloned.1.call-update) | async-done | bytes 524304 | tf_op jit(solution)/shard_map/psum | solution.py:21
  326.7 44.8 %fusion = f32[32,4096]{1,0:T(8,128)} fusion(f32[4096,4096]{1,0:T(8,128)} %param.3, f32[32,4096]{1,0:T(8,128)S(1)} %copy-done, f32[32,4096]{1,0:T(8,128)} %all-reduce.14.cloned.1.call-done), kind=kOutput, calls=%fused_computation | convolution fusion | flops 6442582016 | bytes 68681728 | tf_op jit(solution)/shard_map/dot_general | solution.py:22
  371.5 0.0 reduce-scatter.6.cloned.1.call-update
  371.6 0.0 all-reduce.16.cloned.1.call-start
  371.6 21.9 %reduce-scatter.6.cloned.1.call-done = f32[32,1024]{1,0:T(8,128)} async-done(((f32[32,4096]{1,0:T(8,128)}), f32[32,1024]{1,0:T(8,128)}) %reduce-scatter.6.cloned.1.call-update) | async-done | bytes 131088 | tf_op jit(solution)/shard_map/reduce_scatter | solution.py:25
  393.5 0.9 dynamic-slice_divide_fusion.1
  394.5 15.6 %all_gather.10 = f32[32,4096]{1,0:T(8,128)S(1)} all-gather(f32[32,1024]{1,0:T(8,128)S(1)} %dynamic-slice_divide_fusion.1), channel_id=1, replica_groups=mesh['groups'=2,'row'=4,'col'=2,'rep'=2] {'row'}, dimensions={1}, use_global_device_ids=true | all-gather | bytes 655360 | tf_op jit(solution)/shard_map/all_gather | solution.py:26
  410.0 66.5 %fusion.8 = f32[32,4096]{1,0:T(8,128)} fusion(f32[32,4096]{1,0:T(8,128)S(1)} %all_gather.10, f32[4096,4096]{1,0:T(8,128)} %param.3), kind=kOutput, calls=%fused_computation.18 | convolution fusion | flops 6442450944 | bytes 68157440 | tf_op jit(solution)/shard_map/dot_general | solution.py:18
  476.5 0.0 all-reduce.16.cloned.1.call-update
  476.6 0.0 all-reduce.18.cloned.1.call-start
  476.6 17.2 %all-reduce.16.cloned.1.call-done = f32[32,4096]{1,0:T(8,128)} async-done(((f32[32,4096]{1,0:T(8,128)}), f32[32,4096]{1,0:T(8,128)}) %all-reduce.16.cloned.1.call-update) | async-done | bytes 524304 | tf_op jit(solution)/shard_map/psum | solution.py:21
  493.8 0.0 all-reduce.18.cloned.1.call-update
  493.8 0.3 reduce-scatter.8.cloned.1.call-start
  494.1 31.9 %all-reduce.18.cloned.1.call-done = f32[32,4096]{1,0:T(8,128)} async-done(((f32[32,4096]{1,0:T(8,128)}), f32[32,4096]{1,0:T(8,128)}) %all-reduce.18.cloned.1.call-update) | async-done | bytes 524304 | tf_op jit(solution)/shard_map/psum | solution.py:21
  525.9 1.1 div.31
  527.1 0.0 copy-start.1
  527.1 45.0 %fusion.9 = f32[32,4096]{1,0:T(8,128)} fusion(f32[32,4096]{1,0:T(8,128)S(1)} %div.31, f32[4096,4096]{1,0:T(8,128)} %param.3), kind=kOutput, calls=%fused_computation.19 | convolution fusion | flops 6442450944 | bytes 68157440 | tf_op jit(solution)/shard_map/dot_general | solution.py:22
  572.1 0.0 reduce-scatter.8.cloned.1.call-update
  572.1 22.0 %reduce-scatter.8.cloned.1.call-done = f32[32,1024]{1,0:T(8,128)} async-done(((f32[32,4096]{1,0:T(8,128)}), f32[32,1024]{1,0:T(8,128)}) %reduce-scatter.8.cloned.1.call-update) | async-done | bytes 131088 | tf_op jit(solution)/shard_map/reduce_scatter | solution.py:25
  594.1 0.0 copy-done.2
  594.1 1.1 abs_reduce_fusion.2
  595.2 15.4 %all_gather.11 = f32[32,4096]{1,0:T(8,128)S(1)} all-gather(f32[32,1024]{1,0:T(8,128)S(1)} %get-tuple-element.9), channel_id=1, replica_groups=mesh['groups'=2,'row'=4,'col'=2,'rep'=2] {'row'}, dimensions={1}, use_global_device_ids=true | all-gather | bytes 655360 | tf_op jit(solution)/shard_map/all_gather | solution.py:26
  610.6 29.5 %all-reduce = (f32[1,32]{1,0:T(1,128)S(1)}, f32[1,32]{1,0:T(1,128)S(1)}, f32[1,32]{1,0:T(1,128)S(1)}) all-reduce(f32[1,32]{1,0:T(1,128)S(1)} %get-tuple-element.10, f32[1,32]{1,0:T(1,128)S(1)} %get-tuple-element.11, f32[1,32]{1,0:T(1,128)S(1)} %multiply_bitcast_fusion.2), channel_id=1, replica_groups=mesh['groups'=2,'row'=4,'col'=2,'rep'=2] {'row','col','rep'}, use_global_device_ids=true, to_apply=%region_14.0 | all-reduce | flops 96 | bytes 768 | tf_op jit(solution)/shard_map/psum | solution.py:28
  640.1 0.6 pad_maximum_fusion
  640.7 0.8 copy.13
  (7 shorter events, 0.0 us)
Async XLA Ops:
  7.2 120.2 %copy-start = (f32[32,4096]{1,0:T(8,128)S(1)}, f32[32,4096]{1,0:T(8,128)}, u32[]{:S(2)}) copy-start(f32[32,4096]{1,0:T(8,128)} %param.4) | copy-start | bytes 1572868
  7.2 88.0 %all-reduce.8.cloned.1.call-start = ((), (), s32[]{:S(2)}) async-start(), calls=%async_computation.3 | async-start | bytes 1048576 | tf_op jit(solution)/shard_map/psum | solution.py:21
  73.7 120.5 %copy-start.4 = (f32[32,4096]{1,0:T(8,128)S(1)}, f32[32,4096]{1,0:T(8,128)}, u32[]{:S(2)}) copy-start(f32[32,4096]{1,0:T(8,128)} %param.5) | copy-start | bytes 1572868
  73.7 53.7 %all-reduce.10.cloned.1.call-start = ((), (), s32[]{:S(2)}) async-start(), calls=%async_computation.4 | async-start | bytes 1048576 | tf_op jit(solution)/shard_map/psum | solution.py:21
  95.2 99.0 %reduce-scatter.4.cloned.1.call-start = ((), (), s32[]{:S(2)}) async-start(), calls=%async_computation.5 | async-start | bytes 655360 | tf_op jit(solution)/shard_map/reduce_scatter | solution.py:25
  172.2 122.4 %all-reduce.12.cloned.1.call-start = ((), (), s32[]{:S(2)}) async-start(), calls=%async_computation.6 | async-start | bytes 1048576 | tf_op jit(solution)/shard_map/psum | solution.py:21
  277.4 49.3 %all-reduce.14.cloned.1.call-start = ((), (), s32[]{:S(2)}) async-start(), calls=%async_computation.7 | async-start | bytes 1048576 | tf_op jit(solution)/shard_map/psum | solution.py:21
  294.7 98.8 %reduce-scatter.6.cloned.1.call-start = ((), (), s32[]{:S(2)}) async-start(), calls=%async_computation.8 | async-start | bytes 655360 | tf_op jit(solution)/shard_map/reduce_scatter | solution.py:25
  371.6 122.2 %all-reduce.16.cloned.1.call-start = ((), (), s32[]{:S(2)}) async-start(), calls=%async_computation.9 | async-start | bytes 1048576 | tf_op jit(solution)/shard_map/psum | solution.py:21
  476.5 117.6 %copy-start.2 = (f32[32,1024]{1,0:T(8,128)S(1)}, f32[32,1024]{1,0:T(8,128)}, u32[]{:S(2)}) copy-start(f32[32,1024]{1,0:T(8,128)} %reduce-scatter.4.cloned.1.call-done) | copy-start | bytes 393220
  476.5 117.6 %copy-start.3 = (f32[32,1024]{1,0:T(8,128)S(1)}, f32[32,1024]{1,0:T(8,128)}, u32[]{:S(2)}) copy-start(f32[32,1024]{1,0:T(8,128)} %reduce-scatter.6.cloned.1.call-done) | copy-start | bytes 393220
  476.6 49.4 %all-reduce.18.cloned.1.call-start = ((), (), s32[]{:S(2)}) async-start(), calls=%async_computation.10 | async-start | bytes 1048576 | tf_op jit(solution)/shard_map/psum | solution.py:21
  493.8 100.3 %reduce-scatter.8.cloned.1.call-start = ((), (), s32[]{:S(2)}) async-start(), calls=%async_computation.11 | async-start | bytes 655360 | tf_op jit(solution)/shard_map/reduce_scatter | solution.py:25
  527.1 114.4 %copy-start.1 = (f32[32,4096]{1,0:T(8,128)}, f32[32,4096]{1,0:T(8,128)S(1)}, u32[]{:S(2)}) copy-start(f32[32,4096]{1,0:T(8,128)S(1)} %div.31) | copy-start | bytes 1572868
Sparse Core Ops, SparseCore 0:
  73.8 21.3 all-reduce.7
  97.5 29.8 all-reduce.9
  172.3 21.8 reduce-scatter.3
  277.6 17.0 all-reduce.11
  296.8 29.8 all-reduce.13
  371.7 21.8 reduce-scatter.5
  476.7 17.0 all-reduce.15
  496.1 29.8 all-reduce.17
  572.3 21.8 reduce-scatter.7
